TPU v7x, 256 devices: a whole 4x4x8 slice. The times are simulated.
256 devices in a mesh: dp: 2 (over core), row: 16 (over x, y), col: 8 (over z).
Axes of the slice: x: 4, y: 4, z: 8, core: 2. Of those that a mesh axis runs over, the one named last changes fastest.
Arguments:
- tokens: bfloat16 [1536, 8192], P('dp', 'row'), may hold values from -6 to 6
- out_grad: bfloat16 [1536, 8192], P('dp', 'row'), may hold values from -6 to 6
- gate_weight: bfloat16 [8192, 14336], P('row', 'col'), may hold values from -0.0625 to 0.0625
- up_weight: bfloat16 [8192, 14336], P('row', 'col'), may hold values from -0.0625 to 0.0625
- down_weight: bfloat16 [14336, 8192], P('col', 'row'), may hold values from -0.046875 to 0.046875
- gate_mask: int32 [64, 112], P('row', 'col'), may hold values from 0 to 1, as said below
- up_mask: int32 [64, 112], P('row', 'col'), may hold values from 0 to 1, as said below
- down_mask: int32 [112, 64], P('col', 'row'), may hold values from 0 to 1, as said below
Outputs:
- output: bfloat16 [1536, 8192], P(('dp', 'col'), 'row')
- token_grad: bfloat16 [1536, 8192], P(('dp', 'col'), 'row')
- gate_grad: bfloat16 [8192, 14336], P('row', 'col')
- up_grad: bfloat16 [8192, 14336], P('row', 'col')
- down_grad: bfloat16 [14336, 8192], P('col', 'row')
Inputs may be any that keep to these rules, and one draw needn't show every extreme that they name: `gate_mask`: one keep flag for each 128 x 128 block of the matrix; the share kept differs from block row to block row. `up_mask`: one keep flag for each 128 x 128 block of the matrix; the share kept differs from block row to block row. `down_mask`: one keep flag for each 128 x 128 block of the matrix; the share kept differs from block column to block column.
All inputs are finite; a program needn't handle non-finite values.
Results may differ from a plain program's by a relative error of at most 0.029.
Values may be sent and summed in bfloat16 or wider, within the bound.
A program may use at most 128 MiB of HBM per device.

v0:
```python
import jax
import jax.numpy as jnp
from jax import lax
from jax.sharding import PartitionSpec as P

BLOCK = 128


def expand(mask_tile):
    return jnp.repeat(jnp.repeat(mask_tile, BLOCK, axis=0), BLOCK, axis=1)


def contract_rows(left_side, right_side):
    return lax.dot_general(
        left_side, right_side, (((0,), (0,)), ((), ())), preferred_element_type=jnp.float32
    )


def contract_cols(left_side, right_side):
    return lax.dot_general(
        left_side, right_side, (((1,), (1,)), ((), ())), preferred_element_type=jnp.float32
    )


def body(tokens, out_grad, gate_weight, up_weight, down_weight, gate_mask, up_mask, down_mask):
    gate_keep = expand(gate_mask)
    up_keep = expand(up_mask)
    down_keep = expand(down_mask)
    gate_eff = gate_weight * gate_keep.astype(jnp.bfloat16)
    up_eff = up_weight * up_keep.astype(jnp.bfloat16)
    down_eff = down_weight * down_keep.astype(jnp.bfloat16)
    gate_part = jnp.dot(tokens, gate_eff, preferred_element_type=jnp.float32)
    up_part = jnp.dot(tokens, up_eff, preferred_element_type=jnp.float32)
    gate_share, up_share = (
        lax.psum_scatter(
            gate_part.astype(jnp.bfloat16), "row", scatter_dimension=0, tiled=True
        ).astype(jnp.float32),
        lax.psum_scatter(
            up_part.astype(jnp.bfloat16), "row", scatter_dimension=0, tiled=True
        ).astype(jnp.float32),
    )
    gate_sig = jax.nn.sigmoid(gate_share)
    silu_gate = gate_share * gate_sig
    hidden_share = (silu_gate * up_share).astype(jnp.bfloat16)
    hidden = lax.all_gather(hidden_share, "row", axis=0, tiled=True)
    output = lax.psum_scatter(
        jnp.dot(hidden, down_eff, preferred_element_type=jnp.float32).astype(jnp.bfloat16),
        "col",
        scatter_dimension=0,
        tiled=True,
    )
    down_local = contract_rows(hidden, out_grad) * down_keep.astype(jnp.float32)
    back_part = contract_cols(out_grad, down_eff)
    back_share = lax.psum_scatter(
        back_part.astype(jnp.bfloat16), "row", scatter_dimension=0, tiled=True
    ).astype(jnp.float32)
    gate_deriv = (back_share * up_share * gate_sig * (1.0 + gate_share * (1.0 - gate_sig))).astype(
        jnp.bfloat16
    )
    up_deriv = (back_share * silu_gate).astype(jnp.bfloat16)
    gate_full, up_full = (
        lax.all_gather(gate_deriv, "row", axis=0, tiled=True),
        lax.all_gather(up_deriv, "row", axis=0, tiled=True),
    )
    token_grad = lax.psum_scatter(
        (contract_cols(gate_full, gate_eff) + contract_cols(up_full, up_eff)).astype(jnp.bfloat16),
        "col",
        scatter_dimension=0,
        tiled=True,
    )
    gate_local = contract_rows(tokens, gate_full) * gate_keep.astype(jnp.float32)
    up_local = contract_rows(tokens, up_full) * up_keep.astype(jnp.float32)
    gate_total, up_total, down_total = (
        lax.psum(gate_local.astype(jnp.bfloat16), "dp").astype(jnp.float32),
        lax.psum(up_local.astype(jnp.bfloat16), "dp").astype(jnp.float32),
        lax.psum(down_local.astype(jnp.bfloat16), "dp").astype(jnp.float32),
    )
    return (
        output,
        token_grad,
        gate_total.astype(jnp.bfloat16),
        up_total.astype(jnp.bfloat16),
        down_total.astype(jnp.bfloat16),
    )


def solution(mesh):
    placed = (
        P("dp", "row"),
        P("dp", "row"),
        P("row", "col"),
        P("row", "col"),
        P("col", "row"),
        P("row", "col"),
        P("row", "col"),
        P("col", "row"),
    )
    return jax.shard_map(
        body,
        mesh=mesh,
        in_specs=placed,
        out_specs=(
            P(("dp", "col"), "row"),
            P(("dp", "col"), "row"),
            P("row", "col"),
            P("row", "col"),
            P("col", "row"),
        ),
        check_vma=False,
    )
```

profile of v0, /device:TPU:2, one launch (start us, length us, event | category | flops | bytes accessed | tf_op | source)
XLA Modules:
  0.0 568.2 jit_solution(9316289985637627538)
XLA Ops:
  8.2 5.1 broadcast_in_dim.35
  16.2 2.9 copy.59
  19.1 2.8 copy.43
  25.2 2.9 copy.55
  28.2 2.8 copy.46
  34.2 2.9 copy.57
  37.2 66.0 %reduce-scatter.20.cloned.1.call-done = bf16[48,1792]{1,0:T(8,128)(2,1)} async-done(((bf16[768,1792]{1,0:T(8,128)(2,1)}), bf16[48,1792]{1,0:T(8,128)(2,1)}) %reduce-scatter.20.cloned.1.call-update) | async-done | bytes 172048 | tf_op jit(solution)/shard_map/reduce_scatter | solution.py:54
  103.2 84.2 %reduce-scatter.16.cloned.1.call-done = bf16[48,1792]{1,0:T(8,128)(2,1)} async-done(((bf16[768,1792]{1,0:T(8,128)(2,1)}), bf16[48,1792]{1,0:T(8,128)(2,1)}) %reduce-scatter.16.cloned.1.call-update) | async-done | bytes 172048 | tf_op jit(solution)/shard_map/reduce_scatter | solution.py:35
  187.5 84.3 %reduce-scatter.18.cloned.1.call-done = bf16[48,1792]{1,0:T(8,128)(2,1)} async-done(((bf16[768,1792]{1,0:T(8,128)(2,1)}), bf16[48,1792]{1,0:T(8,128)(2,1)}) %reduce-scatter.18.cloned.1.call-update) | async-done | bytes 172048 | tf_op jit(solution)/shard_map/reduce_scatter | solution.py:38
  275.7 48.8 %all-gather.6.cloned.1.call-done = bf16[768,1792]{1,0:T(8,128)(2,1)} async-done(((bf16[48,1792]{1,0:T(8,128)(2,1)}), bf16[768,1792]{1,0:T(8,128)(2,1)}) %all-gather.6.cloned.1.call-update) | async-done | bytes 2752528 | tf_op jit(solution)/shard_map/all_gather | solution.py:62
  324.5 4.7 fusion.2
  329.2 48.4 %all-gather.8.cloned.1.call-done = bf16[768,1792]{1,0:T(8,128)(2,1)} async-done(((bf16[48,1792]{1,0:T(8,128)(2,1)}), bf16[768,1792]{1,0:T(8,128)(2,1)}) %all-gather.8.cloned.1.call-update) | async-done | bytes 2752528 | tf_op jit(solution)/shard_map/all_gather | solution.py:63
  377.6 4.7 fusion.1
  382.3 48.4 %all-gather.4.cloned.1.call-done = bf16[768,1792]{1,0:T(8,128)(2,1)} async-done(((bf16[48,1792]{1,0:T(8,128)(2,1)}), bf16[768,1792]{1,0:T(8,128)(2,1)}) %all-gather.4.cloned.1.call-update) | async-done | bytes 2752528 | tf_op jit(solution)/shard_map/all_gather | solution.py:45
  430.8 2.2 broadcast_in_dim.41
  433.0 2.9 fusion
  436.0 5.5 convolution_convert_fusion.3
  441.6 3.2 fusion.18
  444.8 2.5 add_convert_fusion
  447.3 29.8 %all-reduce.3.cloned.1.call-done = (bf16[512,1792]{0,1:T(8,128)(2,1)}, bf16[512,1792]{0,1:T(8,128)(2,1)}, bf16[1792,512]{1,0:T(8,128)(2,1)}) async-done(((bf16[512,1792]{0,1:T(8,128)(2,1)}, bf16[512,1792]{0,1:T(8,128)(2,1)}, bf16[1792,512]{1,0:T(8,128)(2,1)}), (bf16[512,1792]{0,1:T(8,128)(2,1)}, bf16[512,1792]{0,1:T(8,128)(2,1)}, bf16[1792,512]{1,0:T(8,128)(2,1)})) %all-reduce.3.cloned.1.call-update) | async-done | bytes 5505040 | tf_op jit(solution)/shard_map/psum | solution.py:74
  477.1 3.8 copy.53
  480.9 3.9 copy.54
  484.8 35.0 %reduce-scatter.12.cloned.1.call-done = bf16[96,512]{1,0:T(8,128)(2,1)} async-done(((bf16[768,512]{1,0:T(8,128)(2,1)}), bf16[96,512]{1,0:T(8,128)(2,1)}) %reduce-scatter.12.cloned.1.call-update) | async-done | bytes 98320 | tf_op jit(solution)/shard_map/reduce_scatter | solution.py:46
  519.9 40.1 %reduce-scatter.14.cloned.1.call-done = bf16[96,512]{1,0:T(8,128)(2,1)} async-done(((bf16[768,512]{1,0:T(8,128)(2,1)}), bf16[96,512]{1,0:T(8,128)(2,1)}) %reduce-scatter.14.cloned.1.call-update) | async-done | bytes 98320 | tf_op jit(solution)/shard_map/reduce_scatter | solution.py:65
  (78 shorter events, 16.2 us)
Async XLA Ops:
  7.2 16.4 %copy-start = (bf16[768,512]{1,0:T(8,128)(2,1)S(1)}, bf16[768,512]{1,0:T(8,128)(2,1)}, u32[]{:S(2)}) copy-start(bf16[768,512]{1,0:T(8,128)(2,1)} %param.8) | copy-start | bytes 2359300
  7.2 96.1 %reduce-scatter.20.cloned.1.call-start = ((), (), s32[]{:S(2)}) async-start(), calls=%async_computation.12 | async-start | bytes 2924544 | tf_op jit(solution)/shard_map/reduce_scatter | solution.py:54
  8.1 6.4 %copy-start.12 = (bf16[1792,512]{1,0:T(8,128)(2,1)S(1)}, bf16[1792,512]{1,0:T(8,128)(2,1)}, u32[]{:S(2)}) copy-start(bf16[1792,512]{1,0:T(8,128)(2,1)} %param.12) | copy-start | bytes 5505028
  8.1 6.4 %copy-start.13 = (bf16[768,512]{1,0:T(8,128)(2,1)S(1)}, bf16[768,512]{1,0:T(8,128)(2,1)}, u32[]{:S(2)}) copy-start(bf16[768,512]{1,0:T(8,128)(2,1)} %param.9) | copy-start | bytes 2359300
  13.3 1.2 copy-start.8
  19.1 2.9 copy-start.9
  19.1 168.4 %reduce-scatter.16.cloned.1.call-start = ((), (), s32[]{:S(2)}) async-start(), calls=%async_computation.10 | async-start | bytes 2924544 | tf_op jit(solution)/shard_map/reduce_scatter | solution.py:35
  22.3 1.2 copy-start.4
  28.1 2.9 copy-start.10
  28.1 243.6 %reduce-scatter.18.cloned.1.call-start = ((), (), s32[]{:S(2)}) async-start(), calls=%async_computation.11 | async-start | bytes 2924544 | tf_op jit(solution)/shard_map/reduce_scatter | solution.py:38
  31.4 1.2 copy-start.5
  37.2 287.3 %all-gather.6.cloned.1.call-start = ((), (), s32[]{:S(2)}) async-start(), calls=%async_computation.7 | async-start | bytes 2924544 | tf_op jit(solution)/shard_map/all_gather | solution.py:62
  273.8 103.8 %all-gather.8.cloned.1.call-start = ((), (), s32[]{:S(2)}) async-start(), calls=%async_computation.8 | async-start | bytes 2924544 | tf_op jit(solution)/shard_map/all_gather | solution.py:63
  274.4 156.3 %all-gather.4.cloned.1.call-start = ((), (), s32[]{:S(2)}) async-start(), calls=%async_computation.5 | async-start | bytes 2924544 | tf_op jit(solution)/shard_map/all_gather | solution.py:45
  275.0 202.1 %all-reduce.3.cloned.1.call-start = ((), (), s32[]{:S(2)}) async-start(), calls=%async_computation.13 | async-start | bytes 11010048 | tf_op jit(solution)/shard_map/psum | solution.py:74
  430.7 2.2 copy-start.11
  430.8 2.2 copy-start.14
  435.9 5.7 copy-start.2
  435.9 83.9 %reduce-scatter.12.cloned.1.call-start = ((), (), s32[]{:S(2)}) async-start(), calls=%async_computation.6 | async-start | bytes 884736 | tf_op jit(solution)/shard_map/reduce_scatter | solution.py:46
  441.5 118.5 %reduce-scatter.14.cloned.1.call-start = ((), (), s32[]{:S(2)}) async-start(), calls=%async_computation.9 | async-start | bytes 884736 | tf_op jit(solution)/shard_map/reduce_scatter | solution.py:65
  441.6 3.3 copy-start.3
  441.6 3.3 copy-start.6
  480.9 79.1 %copy-start.7 = (bf16[1792,512]{1,0:T(8,128)(2,1)S(1)}, bf16[1792,512]{1,0:T(8,128)(2,1)}, u32[]{:S(2)}) copy-start(bf16[1792,512]{1,0:T(8,128)(2,1)} %get-tuple-element.41) | copy-start | bytes 5505028
  560.0 1.7 copy-start.1
Sparse Core Ops, SparseCore 0:
  19.2 84.0 reduce-scatter.19
  106.8 80.5 reduce-scatter.15
  191.1 80.5 reduce-scatter.17
  274.1 50.4 all-gather.5
  326.9 50.6 all-gather.7
  379.9 50.6 all-gather.3
  436.0 41.0 all-reduce.2
  480.2 39.6 reduce-scatter.11
  523.0 36.9 reduce-scatter.13
where the time goes:
time: 569 us; the launch traced here: 568 us
  waiting for transfers between devices  486 us (85%)
  local copies, waits for them, and re-layouts  35.8 us (6%)
  matrix products  28.4 us (5%)
  between operations  14.2 us (2%)
    reduce_scatter x1, waiting for transfers between devices, body(): lax.psum_scatter(up_part.astype(jnp.bfloat16), 'row', scatter_dimension=0...  84.3 us
    reduce_scatter x1, waiting for transfers between devices, body(): lax.psum_scatter(gate_part.astype(jnp.bfloat16), 'row', scatter_dimension...  84.2 us
    reduce_scatter x1, waiting for transfers between devices, body(): lax.psum_scatter(back_part.astype(jnp.bfloat16), 'row', scatter_dimension...  66 us
    all_gather x1, waiting for transfers between devices, body(): lax.all_gather(gate_deriv, 'row', axis=0, tiled=True)  48.8 us
    all_gather x1, waiting for transfers between devices, body(): hidden = lax.all_gather(hidden_share, 'row', axis=0, tiled=True)  48.4 us
    all_gather x1, waiting for transfers between devices, body(): lax.all_gather(up_deriv, 'row', axis=0, tiled=True)  48.4 us
    reduce_scatter x1, waiting for transfers between devices, body(): lax.psum_scatter((contract_cols(gate_full, gate_eff) + contract_cols(up_f...  40.1 us
    reduce_scatter x1, waiting for transfers between devices, body(): lax.psum_scatter(jnp.dot(hidden, down_eff, preferred_element_type=jnp.flo...  35 us
  transfers between devices with their start and end apart: 9, of which 9 were waited for; matrix products, arithmetic and copies ran while one was open for 8% of the time, Pallas kernels for 0%

commit v1 on v0

v1 whole, which is shorter than its diff:
```python
import jax
import jax.numpy as jnp
from jax import lax
from jax.experimental import pallas as pl
from jax.experimental.pallas import tpu as pltpu
from jax.sharding import PartitionSpec as P

BLOCK = 128
F32 = jnp.float32
BF16 = jnp.bfloat16
MESH = pl.DeviceIdType.MESH

TOK = 768
DIM = 512
FF = 1792
HALF = FF // 2
BIG = TOK // 4
SMALL = BIG // 4
NZ = 8
ZROWS = TOK // NZ

NN = (((1,), (0,)), ((), ()))
NT = (((1,), (1,)), ((), ()))
TN = (((0,), (0,)), ((), ()))


def dot(a, b, dims=NN):
    return lax.dot_general(a, b, dims, preferred_element_type=F32)


def rows(start, size):
    return pl.ds(pl.multiple_of(start, 16), size)


def kernel(
    x_hbm, dy_hbm, gw_hbm, uw_hbm, dw_hbm, gm, um, dm,
    out_ref, dx_ref, gg_hbm, ug_hbm, dg_hbm,
    x, dy, xt, w, wd, part, q, near1, fin1, near2, fin2, share, full, d, dr, dd, ddr, o, zin, acc,
    ssem, rsem, lsem,
):
    row = lax.axis_index("row")
    zz = lax.axis_index("col")
    core = lax.axis_index("dp")
    cx, cy = row // 4, row % 4

    def rid(a, b):
        return lax.rem(a, 4) * 4 + lax.rem(b, 4)

    xm, xp = rid(cx + 3, cy), rid(cx + 1, cy)
    ym, yp = rid(cx, cy + 3), rid(cx, cy + 1)
    ring1 = ((cx, xm, xp), (cy, ym, yp))
    ring2 = ((cy, ym, yp), (cx, xm, xp))

    loads = {}

    def load(key, src, dst, i):
        cp = pltpu.make_async_copy(src, dst, lsem.at[i])
        cp.start()
        loads[key] = cp

    load("x", x_hbm, x, 0)
    load(("w", 0, 0), gw_hbm.at[:, pl.ds(0, HALF)], w.at[0, 0], 1)
    load(("w", 0, 1), gw_hbm.at[:, pl.ds(HALF, HALF)], w.at[0, 1], 2)
    load(("w", 1, 0), uw_hbm.at[:, pl.ds(0, HALF)], w.at[1, 0], 3)
    load(("w", 1, 1), uw_hbm.at[:, pl.ds(HALF, HALF)], w.at[1, 1], 4)
    load("dy", dy_hbm, dy, 5)
    load(("wd", 0), dw_hbm.at[pl.ds(0, HALF), :], wd.at[0], 6)
    load(("wd", 1), dw_hbm.at[pl.ds(HALF, HALF), :], wd.at[1], 7)

    barrier = pltpu.get_barrier_semaphore()
    for r in (xm, xp, ym, yp):
        pl.semaphore_signal(barrier, inc=1, device_id={"row": r}, device_id_type=MESH)
    pl.semaphore_signal(barrier, inc=1, device_id={"dp": 1 - core}, device_id_type=MESH)
    for k in range(1, NZ):
        pl.semaphore_signal(
            barrier, inc=1, device_id={"col": lax.rem(zz + k, NZ)}, device_id_type=MESH
        )
    pl.semaphore_wait(barrier, 4 + 1 + NZ - 1)

    sent = {}

    def send(key, src, dst, where):
        i = len(sent)
        cp = pltpu.make_async_remote_copy(
            src_ref=src, dst_ref=dst, send_sem=ssem.at[i], recv_sem=rsem.at[i],
            device_id=where, device_id_type=MESH,
        )
        cp.start()
        sent[key] = cp

    def arrived(*key):
        sent[key].wait_recv()

    def mask_cols(ref, mask, h):
        def step(j, _):
            c = pl.ds(pl.multiple_of(j * BLOCK, BLOCK), BLOCK)
            for i in range(DIM // BLOCK):
                r = pl.ds(i * BLOCK, BLOCK)
                keep = mask[i, h * 7 + j].astype(F32)
                ref[r, c] = (ref[r, c].astype(F32) * keep).astype(BF16)
            return 0

        lax.fori_loop(0, 7, step, 0)

    def mask_rows(ref, mask, h):
        def step(j, _):
            r = pl.ds(pl.multiple_of(j * BLOCK, BLOCK), BLOCK)
            for i in range(DIM // BLOCK):
                c = pl.ds(i * BLOCK, BLOCK)
                keep = mask[h * 7 + j, i].astype(F32)
                ref[r, c] = (ref[r, c].astype(F32) * keep).astype(BF16)
            return 0

        lax.fori_loop(0, 7, step, 0)

    def tiles(fn):
        def step(j, _):
            fn(pl.multiple_of(j * 256, 256), 256)
            return 0

        lax.fori_loop(0, 3, step, 0)
        fn(768, 128)

    def add_into(dst, dst_row, terms, n):
        def step(j, _):
            total = None
            for ref, at in terms:
                v = ref[rows(at + j * 48, 48), :].astype(F32)
                total = v if total is None else total + v
            dst[rows(dst_row + j * 48, 48), :] = total.astype(dst.dtype)
            return 0

        lax.fori_loop(0, n // 48, step, 0)

    def first_sends(tag, a, h, src, ring, near, fin, size, cut):
        c, m, p = ring
        far, lo, hi = lax.rem(c + 2, 4) * size, lax.rem(c + 3, 4) * size, lax.rem(c + 1, 4) * size
        rest = size - cut
        send((tag, a, h, "m1"), src.at[rows(far, cut), :], near.at[1, pl.ds(0, cut), :], {"row": m})
        send((tag, a, h, "p1"), src.at[rows(far + cut, rest), :], near.at[0, pl.ds(0, rest), :], {"row": p})
        send((tag, a, h, "m2"), src.at[rows(lo + cut, rest), :], fin.at[1, pl.ds(cut, rest), :], {"row": m})
        send((tag, a, h, "p2"), src.at[rows(hi, cut), :], fin.at[0, pl.ds(0, cut), :], {"row": p})

    def second_sends(tag, a, h, src, ring, near, fin, size, cut, adder):
        c, m, p = ring
        lo, hi = lax.rem(c + 3, 4) * size, lax.rem(c + 1, 4) * size
        rest = size - cut
        arrived(tag, a, h, "m1")
        adder(src, lo, near.at[1], cut)
        send((tag, a, h, "m3"), src.at[rows(lo, cut), :], fin.at[1, pl.ds(0, cut), :], {"row": m})
        arrived(tag, a, h, "p1")
        adder(src, hi + cut, near.at[0], rest)
        send((tag, a, h, "p3"), src.at[rows(hi + cut, rest), :], fin.at[0, pl.ds(cut, rest), :], {"row": p})

    def last_arrivals(tag, a, h):
        for k in ("m2", "p2", "m3", "p3"):
            arrived(tag, a, h, k)

    def add_big(src, at, near, n):
        add_into(src, at, ((src, at), (near, 0)), n)

    def add_small(src, at, near, n):
        src[rows(at, n), :] = (
            src[rows(at, n), :].astype(F32) + near[pl.ds(0, n), :].astype(F32)
        ).astype(BF16)

    def cut2(a, h):
        return 32 if (a + h) % 2 == 0 else 16

    def s0(a, h):
        dst = part.at[a, h]
        if a < 2:
            loads[("w", a, h)].wait()
            mask_cols(w.at[a, h], (gm, um)[a], h)

            def tile(n, size):
                c = pl.ds(n, size)
                dst[:, c] = dot(x[...], w[a, h, :, c]).astype(BF16)
        else:
            loads[("wd", h)].wait()
            mask_rows(wd.at[h], dm, h)

            def tile(n, size):
                c = pl.ds(n, size)
                dst[:, c] = dot(dy[...], wd[h, c, :], NT).astype(BF16)

        tiles(tile)
        first_sends("r1", a, h, dst, ring1[h], near1.at[a, h], fin1.at[a, h], BIG, BIG // 2)

    def s1(a, h):
        second_sends(
            "r1", a, h, part.at[a, h], ring1[h], near1.at[a, h], fin1.at[a, h], BIG, BIG // 2, add_big
        )

    def s2(a, h):
        last_arrivals("r1", a, h)
        add_into(
            q.at[a, h], 0,
            ((part.at[a, h], ring1[h][0] * BIG), (fin1.at[a, h, 0], 0), (fin1.at[a, h, 1], 0)), BIG,
        )
        first_sends("r2", a, h, q.at[a, h], ring2[h], near2.at[a, h], fin2.at[a, h], SMALL, cut2(a, h))

    def s3(a, h):
        second_sends(
            "r2", a, h, q.at[a, h], ring2[h], near2.at[a, h], fin2.at[a, h], SMALL, cut2(a, h), add_small
        )

    def s4(a, h):
        last_arrivals("r2", a, h)
        share[a, h] = (
            q[a, h, rows(ring2[h][0] * SMALL, SMALL), :].astype(F32)
            + fin2[a, h, 0].astype(F32)
            + fin2[a, h, 1].astype(F32)
        )

    def own(h):
        return ring1[h][0] * BIG + ring2[h][0] * SMALL

    def gather_sends(tag, g, h, ring, base, size):
        c, m, p = ring
        here = full.at[g, h, rows(base + c * size, size), :]
        send((tag, g, h, "m1"), here, here, {"row": m})
        send((tag, g, h, "p1"), here, here, {"row": p})

    def gather_passes(tag, g, h, ring, base, size, cut):
        c, m, p = ring
        lo, hi = lax.rem(c + 3, 4) * size, lax.rem(c + 1, 4) * size
        arrived(tag, g, h, "p1")
        there = full.at[g, h, rows(base + lo, cut), :]
        send((tag, g, h, "p2"), there, there, {"row": p})
        arrived(tag, g, h, "m1")
        there = full.at[g, h, rows(base + hi + cut, size - cut), :]
        send((tag, g, h, "m2"), there, there, {"row": m})

    def s5(g, h):
        gather_sends("g2", g, h, ring2[h], ring1[h][0] * BIG, SMALL)

    def s6(g, h):
        gather_passes("g2", g, h, ring2[h], ring1[h][0] * BIG, SMALL, cut2(g, h))

    def s7(g, h):
        arrived("g2", g, h, "p2")
        arrived("g2", g, h, "m2")
        gather_sends("g1", g, h, ring1[h], 0, BIG)

    def s8(g, h):
        gather_passes("g1", g, h, ring1[h], 0, BIG, BIG // 2)

    def s9(g, h):
        arrived("g1", g, h, "p2")
        arrived("g1", g, h, "m2")

    def make_hidden(h):
        gate, up = share[0, h], share[1, h]
        full[0, h, rows(own(h), SMALL), :] = (gate * jax.nn.sigmoid(gate) * up).astype(BF16)

    def make_grads(h):
        gate, up, back = share[0, h], share[1, h], share[2, h]
        sig = jax.nn.sigmoid(gate)
        full[1, h, rows(own(h), SMALL), :] = (
            back * up * sig * (1.0 + gate * (1.0 - sig))
        ).astype(BF16)
        full[2, h, rows(own(h), SMALL), :] = (back * (gate * sig)).astype(BF16)

    def scatter_z(k):
        for s in range(1, NZ):
            peer = lax.rem(zz + s, NZ)
            send(("z", k, s), o.at[k, rows(peer * ZROWS, ZROWS), :], zin.at[k, s - 1], {"col": peer})

    def finish_z(k, ref):
        for s in range(1, NZ):
            arrived("z", k, s)
        total = o[k, rows(zz * ZROWS, ZROWS), :].astype(F32)
        for s in range(1, NZ):
            total = total + zin[k, s - 1].astype(F32)
        ref[...] = total.astype(BF16)

    def out_part():
        def step(j, _):
            r = rows(j * 384, 384)
            o[0, r, :] = (dot(full[0, 0, r, :], wd[0]) + dot(full[0, 1, r, :], wd[1])).astype(BF16)
            return 0

        lax.fori_loop(0, 2, step, 0)
        scatter_z(0)

    def dx_part(g):
        def step(j, _):
            r = rows(j * 384, 384)
            v = dot(full[g, 0, r, :], w[g - 1, 0], NT) + dot(full[g, 1, r, :], w[g - 1, 1], NT)
            if g == 1:
                acc[r, :] = v
            else:
                o[1, r, :] = (acc[r, :] + v).astype(BF16)
            return 0

        lax.fori_loop(0, 2, step, 0)
        if g == 2:
            scatter_z(1)

    def grad_down(h):
        def tile(n, size):
            v = dot(full[0, h, :, pl.ds(n, size)], dy[...], TN)
            for jj in range(size // BLOCK):
                for i in range(DIM // BLOCK):
                    keep = dm[h * 7 + n // BLOCK + jj, i].astype(F32)
                    c = pl.ds(i * BLOCK, BLOCK)
                    dd[h, pl.ds(n + jj * BLOCK, BLOCK), c] = (
                        v[jj * BLOCK : (jj + 1) * BLOCK, i * BLOCK : (i + 1) * BLOCK] * keep
                    ).astype(BF16)

        tiles(tile)
        send(("d", 2, h), dd.at[h], ddr.at[h], {"dp": 1 - core})

    def grad_cols(a, h):
        mask = (gm, um)[a]

        def tile(n, size):
            v = dot(xt[...], full[a + 1, h, :, pl.ds(n, size)])
            for jj in range(size // BLOCK):
                for i in range(DIM // BLOCK):
                    keep = mask[i, h * 7 + n // BLOCK + jj].astype(F32)
                    r = pl.ds(i * BLOCK, BLOCK)
                    d[a, h, r, pl.ds(n + jj * BLOCK, BLOCK)] = (
                        v[i * BLOCK : (i + 1) * BLOCK, jj * BLOCK : (jj + 1) * BLOCK] * keep
                    ).astype(BF16)

        tiles(tile)
        send(("d", a, h), d.at[a, h], dr.at[a, h], {"dp": 1 - core})

    stores = []

    def finish_grad(a, h):
        arrived("d", a, h)
        sent[("d", a, h)].wait_send()
        mine, other = (d.at[a, h], dr.at[a, h]) if a < 2 else (dd.at[h], ddr.at[h])
        n = DIM if a < 2 else HALF

        def step(j, _):
            r = rows(j * 64, 64)
            mine[r, :] = (mine[r, :].astype(F32) + other[r, :].astype(F32)).astype(BF16)
            return 0

        lax.fori_loop(0, n // 64, step, 0)
        if a < 2:
            target = (gg_hbm, ug_hbm)[a].at[:, pl.ds(h * HALF, HALF)]
        else:
            target = dg_hbm.at[pl.ds(h * HALF, HALF), :]
        cp = pltpu.make_async_copy(mine, target, lsem.at[8 + a * 2 + h])
        cp.start()
        stores.append(cp)

    def both(fn, *args):
        fn(*args, 0)
        fn(*args, 1)

    loads["x"].wait()
    both(s0, 0)
    both(s0, 1)
    both(s1, 0)
    loads["dy"].wait()
    both(s0, 2)
    both(s1, 1)
    both(s2, 0)
    both(s1, 2)
    both(s3, 0)
    both(s2, 1)
    both(s4, 0)
    both(s3, 1)
    both(s2, 2)
    both(s4, 1)
    both(make_hidden)
    both(s5, 0)
    both(s3, 2)
    both(s6, 0)
    both(s4, 2)
    both(make_grads)
    both(s5, 1)
    both(s7, 0)
    both(s5, 2)
    both(s6, 1)
    both(s6, 2)
    for i in range(DIM // BLOCK):
        xt[pl.ds(i * BLOCK, BLOCK), :] = x[:, pl.ds(i * BLOCK, BLOCK)].T
    both(s7, 1)
    both(s8, 0)
    both(s7, 2)
    both(s9, 0)
    out_part()
    both(s8, 1)
    both(grad_down)
    both(s8, 2)
    both(s9, 1)
    dx_part(1)
    both(grad_cols, 0)
    both(finish_grad, 2)
    both(s9, 2)
    dx_part(2)
    both(grad_cols, 1)
    both(finish_grad, 0)
    finish_z(0, out_ref)
    both(finish_grad, 1)
    finish_z(1, dx_ref)
    for key, cp in sent.items():
        if key[0] != "d":
            cp.wait_send()
    for cp in stores:
        cp.wait()


N_SENDS = 3 * 2 * 2 * 6 + 3 * 2 * 2 * 4 + 2 * (NZ - 1) + 6


def body(tokens, out_grad, gate_weight, up_weight, down_weight, gate_mask, up_mask, down_mask):
    hbm = pl.BlockSpec(memory_space=pl.ANY)
    smem = pl.BlockSpec(memory_space=pltpu.SMEM)
    vmem = pl.BlockSpec(memory_space=pltpu.VMEM)
    return pl.pallas_call(
        kernel,
        out_shape=(
            jax.ShapeDtypeStruct((ZROWS, DIM), BF16),
            jax.ShapeDtypeStruct((ZROWS, DIM), BF16),
            jax.ShapeDtypeStruct((DIM, FF), BF16),
            jax.ShapeDtypeStruct((DIM, FF), BF16),
            jax.ShapeDtypeStruct((FF, DIM), BF16),
        ),
        in_specs=[hbm] * 5 + [smem] * 3,
        out_specs=(vmem, vmem, hbm, hbm, hbm),
        scratch_shapes=[
            pltpu.VMEM((TOK, DIM), BF16),
            pltpu.VMEM((TOK, DIM), BF16),
            pltpu.VMEM((DIM, TOK), BF16),
            pltpu.VMEM((2, 2, DIM, HALF), BF16),
            pltpu.VMEM((2, HALF, DIM), BF16),
            pltpu.VMEM((3, 2, TOK, HALF), BF16),
            pltpu.VMEM((3, 2, BIG, HALF), BF16),
            pltpu.VMEM((3, 2, 2, BIG // 2, HALF), BF16),
            pltpu.VMEM((3, 2, 2, BIG, HALF), BF16),
            pltpu.VMEM((3, 2, 2, 32, HALF), BF16),
            pltpu.VMEM((3, 2, 2, SMALL, HALF), BF16),
            pltpu.VMEM((3, 2, SMALL, HALF), F32),
            pltpu.VMEM((3, 2, TOK, HALF), BF16),
            pltpu.VMEM((2, 2, DIM, HALF), BF16),
            pltpu.VMEM((2, 2, DIM, HALF), BF16),
            pltpu.VMEM((2, HALF, DIM), BF16),
            pltpu.VMEM((2, HALF, DIM), BF16),
            pltpu.VMEM((2, TOK, DIM), BF16),
            pltpu.VMEM((2, NZ - 1, ZROWS, DIM), BF16),
            pltpu.VMEM((TOK, DIM), F32),
            pltpu.SemaphoreType.DMA((N_SENDS,)),
            pltpu.SemaphoreType.DMA((N_SENDS,)),
            pltpu.SemaphoreType.DMA((14,)),
        ],
        compiler_params=pltpu.CompilerParams(
            collective_id=0, has_side_effects=True, vmem_limit_bytes=66_000_000
        ),
    )(tokens, out_grad, gate_weight, up_weight, down_weight, gate_mask, up_mask, down_mask)


def solution(mesh):
    placed = (
        P("dp", "row"),
        P("dp", "row"),
        P("row", "col"),
        P("row", "col"),
        P("col", "row"),
        P("row", "col"),
        P("row", "col"),
        P("col", "row"),
    )
    return jax.shard_map(
        body,
        mesh=mesh,
        in_specs=placed,
        out_specs=(
            P(("dp", "col"), "row"),
            P(("dp", "col"), "row"),
            P("row", "col"),
            P("row", "col"),
            P("col", "row"),
        ),
        check_vma=False,
    )
```

time: 569 us -> 138 us (0.24)
  waiting for transfers between devices: 486 us -> 0 us
  Pallas kernels: 0 us -> 126 us
  matrix products: 28.4 us -> 0 us
  local copies, waits for them, and re-layouts: 35.8 us -> 10.8 us
  between operations: 14.2 us -> 0.64 us
    reduce_scatter x5 -> x0, waiting for transfers between devices: 310 us -> none  [the longest x1 84.3 us: body(): lax.psum_scatter(up_part.astype(jnp.bfloat16), 'row', scatter_dimension=0...]
    all_gather x3 -> x0, waiting for transfers between devices: 146 us -> none  [the longest x1 48.8 us: body(): lax.all_gather(gate_deriv, 'row', axis=0, tiled=True)]
    pallas_call x0 -> x1, Pallas kernels: none -> 126 us  [body(): pl.pallas_call(kernel, out_shape=(jax.ShapeDtypeStruct((ZROWS, DIM), BF16...]
    psum x1 -> x0, waiting for transfers between devices: 29.8 us -> none  [body(): lax.psum(gate_local.astype(jnp.bfloat16), 'dp').astype(jnp.float32)]
    dot_general x9 -> x0, matrix products: 28.4 us -> none  [the longest x3 12.3 us: contract_rows(): lax.dot_general(left_side, right_side, (((0,), (0,)), ((), ())), preferre...]
    unnamed x50 -> x10, local copies, waits for them, and re-layouts: 27.8 us -> 10.8 us
    broadcast_in_dim x4 -> x0, local copies, waits for them, and re-layouts: 7.42 us -> none  [expand(): return jnp.repeat(jnp.repeat(mask_tile, BLOCK, axis=0), BLOCK, axis=1)]
  transfers between devices with their start and end apart: 9 -> 0, of which waited for: 9 -> 0; matrix products, arithmetic and copies ran while one was open for 8% -> 0% of each run, Pallas kernels for 0% -> 0%
where the time goes in v1:
time: 138 us; the launch traced here: 137 us
  Pallas kernels  126 us (91%)
  local copies, waits for them, and re-layouts  10.8 us (8%)
    pallas_call x1, Pallas kernels, body(): pl.pallas_call(kernel, out_shape=(jax.ShapeDtypeStruct((ZROWS, DIM), BF16...  126 us
    unnamed x10, local copies, waits for them, and re-layouts  10.8 us

profile of v1, /device:TPU:2, one launch (start us, length us, event | category | flops | bytes accessed | tf_op | source)
XLA Modules:
  0.0 137.2 jit_solution(14800580747349117319)
XLA Ops:
  0.6 1.4 copy.13.dm
  2.0 125.8 %shard_map.119 = (bf16[96,512]{1,0:T(8,128)(2,1)}, bf16[96,512]{1,0:T(8,128)(2,1)}, bf16[512,1792]{1,0:T(8,128)(2,1)}, bf16[512,1792]{1,0:T(8,128)(2,1)}, bf16[1792,512]{1,0:T(8,128)(2,1)}) custom-call(bf16[768,512]{1,0:T(8,128)(2,1)} %x_hbm.1, bf16[768,512]{1,0:T(8,128)(2,1)} %dy_hbm.1, bf16[512,1792]{1,0:T(8,128)(2,1)} %gw_hbm.1, ...), custom_call_target="tpu_custom_call" | custom-call | tf_op jit(solution)/shard_map/pallas_call | solution.py:418
  127.8 1.5 %copy.19 = bf16[96,512]{1,0:T(8,128)(2,1)} copy(bf16[96,512]{1,0:T(8,128)(2,1)} %get-tuple-element.10) | data formatting | bytes 196608
  129.3 1.5 %copy.20 = bf16[96,512]{1,0:T(8,128)(2,1)} copy(bf16[96,512]{1,0:T(8,128)(2,1)} %get-tuple-element.11) | data formatting | bytes 196608
  130.9 0.0 copy-start.1
  130.9 3.0 %copy.21 = bf16[512,1792]{1,0:T(8,128)(2,1)} copy(bf16[512,1792]{1,0:T(8,128)(2,1)} %get-tuple-element.12) | data formatting | bytes 3670016
  133.9 0.0 copy-done.1
  133.9 0.0 copy-start
  133.9 1.2 copy.22
  135.1 0.9 copy-done
  136.0 1.2 copy.23
Async XLA Ops:
  130.9 3.0 %copy-start.1 = (bf16[512,1792]{1,0:T(8,128)(2,1)S(1)}, bf16[512,1792]{1,0:T(8,128)(2,1)}, u32[]{:S(2)}) copy-start(bf16[512,1792]{1,0:T(8,128)(2,1)} %get-tuple-element.13) | copy-start | bytes 5505028
  133.9 2.2 %copy-start = (bf16[1792,512]{1,0:T(8,128)(2,1)S(1)}, bf16[1792,512]{1,0:T(8,128)(2,1)}, u32[]{:S(2)}) copy-start(bf16[1792,512]{1,0:T(8,128)(2,1)} %get-tuple-element.14) | copy-start | bytes 5505028

commit v2 on v1

v2 whole, which is shorter than its diff:
```python
import jax
import jax.numpy as jnp
from jax import lax
from jax.experimental import pallas as pl
from jax.experimental.pallas import tpu as pltpu
from jax.sharding import PartitionSpec as P

BLOCK = 128
VMEM_LIMIT = 49000000
F32 = jnp.float32
BF16 = jnp.bfloat16
MESH = pl.DeviceIdType.MESH

TOK = 768
DIM = 512
FF = 1792
HALF = FF // 2
BIG = TOK // 4
SMALL = BIG // 4
NZ = 8
ZROWS = TOK // NZ

NN = (((1,), (0,)), ((), ()))
NT = (((1,), (1,)), ((), ()))
TN = (((0,), (0,)), ((), ()))


def dot(a, b, dims=NN):
    return lax.dot_general(a, b, dims, preferred_element_type=F32)


def rows(start, size):
    return pl.ds(pl.multiple_of(start, 16), size)


def kernel(
    x_hbm, dy_hbm, gw_hbm, uw_hbm, dw_hbm, gm, um, dm,
    out_ref, dx_ref, gg, ug, dg,
    x, dy, xt, w, wd, part, q, near1, fin1, near2, fin2, share, full, dr, ddr, o, zin, odx, zdx, acc,
    ssem, rsem, lsem,
):
    row = lax.axis_index("row")
    zz = lax.axis_index("col")
    core = lax.axis_index("dp")
    cx, cy = row // 4, row % 4

    def rid(a, b):
        return lax.rem(a, 4) * 4 + lax.rem(b, 4)

    xm, xp = rid(cx + 3, cy), rid(cx + 1, cy)
    ym, yp = rid(cx, cy + 3), rid(cx, cy + 1)
    ring1 = ((cx, xm, xp), (cy, ym, yp))
    ring2 = ((cy, ym, yp), (cx, xm, xp))

    loads = {}
    loaded = set()

    def load(key, src, dst, i):
        cp = pltpu.make_async_copy(src, dst, lsem.at[i])
        cp.start()
        loads[key] = cp

    load("x", x_hbm, x, 0)
    load(("w", 0, 0), gw_hbm.at[:, pl.ds(0, HALF)], w.at[0, 0], 1)
    load(("w", 0, 1), gw_hbm.at[:, pl.ds(HALF, HALF)], w.at[0, 1], 2)
    load(("w", 1, 0), uw_hbm.at[:, pl.ds(0, HALF)], w.at[1, 0], 3)
    load(("w", 1, 1), uw_hbm.at[:, pl.ds(HALF, HALF)], w.at[1, 1], 4)
    load("dy", dy_hbm, dy, 5)
    load(("wd", 0), dw_hbm.at[pl.ds(0, HALF), :], wd.at[0], 6)
    load(("wd", 1), dw_hbm.at[pl.ds(HALF, HALF), :], wd.at[1], 7)

    barrier = pltpu.get_barrier_semaphore()
    for r in (xm, xp, ym, yp):
        pl.semaphore_signal(barrier, inc=1, device_id={"row": r}, device_id_type=MESH)
    pl.semaphore_signal(barrier, inc=1, device_id={"dp": 1 - core}, device_id_type=MESH)
    for k in range(1, NZ):
        pl.semaphore_signal(
            barrier, inc=1, device_id={"col": lax.rem(zz + k, NZ)}, device_id_type=MESH
        )
    pl.semaphore_wait(barrier, 4 + 1 + NZ - 1)

    sent = {}

    def send(key, src, dst, where):
        i = len(sent)
        cp = pltpu.make_async_remote_copy(
            src_ref=src, dst_ref=dst, send_sem=ssem.at[i], recv_sem=rsem.at[i],
            device_id=where, device_id_type=MESH,
        )
        cp.start()
        sent[key] = cp

    got = set()

    def arrived(*key):
        got.add(key)
        sent[key].wait_recv()

    def splat(flag):
        return jnp.full((BLOCK, BLOCK), flag.astype(F32), F32).astype(BF16)

    def mask_cols(ref, mask, h):
        def step(j, _):
            c = pl.ds(pl.multiple_of(j * BLOCK, BLOCK), BLOCK)
            for i in range(DIM // BLOCK):
                r = pl.ds(i * BLOCK, BLOCK)
                ref[r, c] = ref[r, c] * splat(mask[i, h * 7 + j])
            return 0

        lax.fori_loop(0, 7, step, 0)

    def mask_rows(ref, mask, h):
        def step(j, _):
            r = pl.ds(pl.multiple_of(j * BLOCK, BLOCK), BLOCK)
            for i in range(DIM // BLOCK):
                c = pl.ds(i * BLOCK, BLOCK)
                ref[r, c] = ref[r, c] * splat(mask[i, h * 7 + j])
            return 0

        lax.fori_loop(0, 7, step, 0)

    def tiles(fn):
        def step(j, _):
            fn(pl.multiple_of(j * 256, 256), 256)
            return 0

        lax.fori_loop(0, 3, step, 0)
        fn(768, 128)

    def add_into(dst, dst_row, terms, n):
        def step(j, _):
            total = None
            for ref, at in terms:
                v = ref[rows(at + j * 48, 48), :].astype(F32)
                total = v if total is None else total + v
            dst[rows(dst_row + j * 48, 48), :] = total.astype(dst.dtype)
            return 0

        lax.fori_loop(0, n // 48, step, 0)

    def near_sends(tag, a, h, src, ring, near, fin, size, cut):
        c, m, p = ring
        far, rest = lax.rem(c + 2, 4) * size, size - cut
        send((tag, a, h, "m1"), src.at[rows(far, cut), :], near.at[1, pl.ds(0, cut), :], {"row": m})
        send((tag, a, h, "p1"), src.at[rows(far + cut, rest), :], near.at[0, pl.ds(0, rest), :], {"row": p})

    def next_sends(tag, a, h, src, ring, near, fin, size, cut):
        c, m, p = ring
        lo, hi, rest = lax.rem(c + 3, 4) * size, lax.rem(c + 1, 4) * size, size - cut
        send((tag, a, h, "m2"), src.at[rows(lo + cut, rest), :], fin.at[1, pl.ds(cut, rest), :], {"row": m})
        send((tag, a, h, "p2"), src.at[rows(hi, cut), :], fin.at[0, pl.ds(0, cut), :], {"row": p})

    def second_sends(tag, a, h, src, ring, near, fin, size, cut, adder):
        c, m, p = ring
        lo, hi = lax.rem(c + 3, 4) * size, lax.rem(c + 1, 4) * size
        rest = size - cut
        arrived(tag, a, h, "m1")
        adder(src, lo, near.at[1], cut)
        send((tag, a, h, "m3"), src.at[rows(lo, cut), :], fin.at[1, pl.ds(0, cut), :], {"row": m})
        arrived(tag, a, h, "p1")
        adder(src, hi + cut, near.at[0], rest)
        send((tag, a, h, "p3"), src.at[rows(hi + cut, rest), :], fin.at[0, pl.ds(cut, rest), :], {"row": p})

    def last_arrivals(tag, a, h):
        for k in ("m2", "p2", "m3", "p3"):
            arrived(tag, a, h, k)

    def add_big(src, at, near, n):
        add_into(src, at, ((src, at), (near, 0)), n)

    def add_small(src, at, near, n):
        src[rows(at, n), :] = (
            src[rows(at, n), :].astype(F32) + near[pl.ds(0, n), :].astype(F32)
        ).astype(BF16)

    def cut2(a, h):
        return 32 if (a + h) % 2 == 0 else 16

    def first_args(a, h):
        return "r1", a, h, part.at[a, h], ring1[h], near1.at[a, h], fin1.at[a, h], BIG, BIG // 2

    def compute(a, h):
        dst = part.at[a, h]
        if a < 2:
            wait_load(("w", a, h))
            mask_cols(w.at[a, h], (gm, um)[a], h)

            def tile(n, size):
                c = pl.ds(n, size)
                dst[:, c] = dot(x[...], w[a, h, :, c]).astype(BF16)
        else:
            wait_load(("wd", h))
            mask_rows(wd.at[h], dm, h)

            def tile(n, size):
                c = pl.ds(n, size)
                dst[:, c] = dot(dy[...], wd[h, c, :], NT).astype(BF16)

        tiles(tile)

    def start_sends(a, h):
        near_sends(*first_args(a, h))
        next_sends(*first_args(a, h))

    def start_gate():
        def chunk(h, k):
            r = rows(lax.rem(ring1[h][0] + k, 4) * BIG, BIG)
            part[0, h, r, :] = dot(x[r, :], w[0, h]).astype(BF16)

        for h in range(2):
            wait_load(("w", 0, h))
            mask_cols(w.at[0, h], gm, h)
            chunk(h, 2)
            near_sends(*first_args(0, h))
        for h in range(2):
            chunk(h, 3)
            chunk(h, 1)
            next_sends(*first_args(0, h))
        for h in range(2):
            chunk(h, 0)

    def s1(a, h):
        second_sends(
            "r1", a, h, part.at[a, h], ring1[h], near1.at[a, h], fin1.at[a, h], BIG, BIG // 2, add_big
        )

    def s2(a, h):
        last_arrivals("r1", a, h)
        add_into(
            q.at[a, h], 0,
            ((part.at[a, h], ring1[h][0] * BIG), (fin1.at[a, h, 0], 0), (fin1.at[a, h, 1], 0)), BIG,
        )
        args = "r2", a, h, q.at[a, h], ring2[h], near2.at[a, h], fin2.at[a, h], SMALL, cut2(a, h)
        near_sends(*args)
        next_sends(*args)

    def s3(a, h):
        second_sends(
            "r2", a, h, q.at[a, h], ring2[h], near2.at[a, h], fin2.at[a, h], SMALL, cut2(a, h), add_small
        )

    def s4(a, h):
        last_arrivals("r2", a, h)
        share[a, h] = (
            q[a, h, rows(ring2[h][0] * SMALL, SMALL), :].astype(F32)
            + fin2[a, h, 0].astype(F32)
            + fin2[a, h, 1].astype(F32)
        )

    def block(g, h, k, b):
        return full.at[g, h, k, b // 2, lax.rem(b, 2)]

    def s5(g, h):
        c, m, p = ring2[h]
        here = block(g, h, ring1[h][0], c)
        send(("g2", g, h, "m1"), here, here, {"row": m})
        send(("g2", g, h, "p1"), here, here, {"row": p})

    def s6(g, h):
        c, m, p = ring2[h]
        k, cut = ring1[h][0], cut2(g, h)
        arrived("g2", g, h, "p1")
        there = block(g, h, k, lax.rem(c + 3, 4)).at[pl.ds(0, cut), :]
        send(("g2", g, h, "p2"), there, there, {"row": p})
        arrived("g2", g, h, "m1")
        there = block(g, h, k, lax.rem(c + 1, 4)).at[pl.ds(cut, SMALL - cut), :]
        send(("g2", g, h, "m2"), there, there, {"row": m})

    def s7(g, e, h):
        if e == 0:
            arrived("g2", g, h, "p2")
            arrived("g2", g, h, "m2")
        c, m, p = ring1[h]
        here = full.at[g, h, c, :, e]
        send(("g1", g, e, h, "m1"), here, here, {"row": m})
        send(("g1", g, e, h, "p1"), here, here, {"row": p})

    def s8(g, e, h):
        c, m, p = ring1[h]
        arrived("g1", g, e, h, "p1")
        there = full.at[g, h, lax.rem(c + 3, 4), 0, e]
        send(("g1", g, e, h, "p2"), there, there, {"row": p})
        arrived("g1", g, e, h, "m1")
        there = full.at[g, h, lax.rem(c + 1, 4), 1, e]
        send(("g1", g, e, h, "m2"), there, there, {"row": m})

    def s9(g, e, h):
        arrived("g1", g, e, h, "p2")
        arrived("g1", g, e, h, "m2")

    def own(g, h):
        return block(g, h, ring1[h][0], ring2[h][0])

    def make_hidden(h):
        gate, up = share[0, h], share[1, h]
        own(0, h)[...] = (gate * jax.nn.sigmoid(gate) * up).astype(BF16)

    def make_grads(h):
        gate, up, back = share[0, h], share[1, h], share[2, h]
        sig = jax.nn.sigmoid(gate)
        own(1, h)[...] = (back * up * sig * (1.0 + gate * (1.0 - sig))).astype(BF16)
        own(2, h)[...] = (back * (gate * sig)).astype(BF16)

    def z_out():
        for i in range(1, NZ):
            peer = lax.rem(zz + i, NZ)
            send(("z", i), o.at[rows(peer * ZROWS, ZROWS), :], zin.at[i - 1], {"col": peer})

    def z_dx(e):
        for i in range(1, NZ):
            peer = lax.rem(zz + i, NZ)
            send(("z", e, i), odx.at[e, peer], zdx.at[e, i - 1], {"col": peer})

    def finish_out():
        for i in range(1, NZ):
            arrived("z", i)
        total = o[rows(zz * ZROWS, ZROWS), :].astype(F32)
        for i in range(1, NZ):
            total = total + zin[i - 1].astype(F32)
        out_ref[...] = total.astype(BF16)

    def finish_dx(e):
        for i in range(1, NZ):
            arrived("z", e, i)
        total = odx[e, zz].astype(F32)
        for i in range(1, NZ):
            total = total + zdx[e, i - 1].astype(F32)
        dx_ref[pl.ds(e * 48, 48), :] = total.astype(BF16)

    def out_part():
        def step(j, _):
            k = pl.ds(2 * j, 2)
            o[rows(j * 384, 384), :] = (
                dot(full[0, 0, k].reshape(384, HALF), wd[0])
                + dot(full[0, 1, k].reshape(384, HALF), wd[1])
            ).astype(BF16)
            return 0

        lax.fori_loop(0, 2, step, 0)
        z_out()

    def dx_part(g, e):
        def term(h):
            return dot(full[g, h, :, :, e].reshape(384, HALF), w[g - 1, h], NT)

        v = term(0) + term(1)
        if g == 1:
            acc[...] = v
        else:
            odx[e] = (acc[...] + v).astype(BF16).reshape(NZ, 48, DIM)
            z_dx(e)

    def mine(a, h):
        part_of = pl.ds(h * HALF, HALF)
        return (gg, ug)[a].at[:, part_of] if a < 2 else dg.at[part_of, :]

    def grad_down(h):
        def tile(n, size):
            v = dot(full[0, h, :, :, :, :, pl.ds(n, size)].reshape(TOK, size), dy[...], TN)
            for jj in range(size // BLOCK):
                for i in range(DIM // BLOCK):
                    keep = dm[i, h * 7 + n // BLOCK + jj].astype(F32)
                    c = pl.ds(i * BLOCK, BLOCK)
                    dg[pl.ds(h * HALF + n + jj * BLOCK, BLOCK), c] = (
                        v[jj * BLOCK : (jj + 1) * BLOCK, i * BLOCK : (i + 1) * BLOCK] * keep
                    ).astype(BF16)

        tiles(tile)
        send(("d", 2, h), mine(2, h), ddr.at[h], {"dp": 1 - core})

    def grad_cols(a, h):
        mask = (gm, um)[a]

        def tile(n, size):
            v = dot(xt[...], full[a + 1, h, :, :, :, :, pl.ds(n, size)].reshape(TOK, size))
            for jj in range(size // BLOCK):
                for i in range(DIM // BLOCK):
                    keep = mask[i, h * 7 + n // BLOCK + jj].astype(F32)
                    r = pl.ds(i * BLOCK, BLOCK)
                    (gg, ug)[a][r, pl.ds(h * HALF + n + jj * BLOCK, BLOCK)] = (
                        v[i * BLOCK : (i + 1) * BLOCK, jj * BLOCK : (jj + 1) * BLOCK] * keep
                    ).astype(BF16)

        tiles(tile)
        send(("d", a, h), mine(a, h), dr.at[a, h], {"dp": 1 - core})

    def finish_grad(a, h):
        arrived("d", a, h)
        sent[("d", a, h)].wait_send()
        here, other = mine(a, h), (dr.at[a, h] if a < 2 else ddr.at[h])
        n = DIM if a < 2 else HALF

        def step(j, _):
            r = rows(j * 64, 64)
            here[r, :] = (here[r, :].astype(F32) + other[r, :].astype(F32)).astype(BF16)
            return 0

        lax.fori_loop(0, n // 64, step, 0)

    def both(fn, *args):
        fn(*args, 0)
        fn(*args, 1)

    def wait_load(name):
        loaded.add(name)
        loads[name].wait()

    def transpose_x():
        for i in range(DIM // BLOCK):
            xt[pl.ds(i * BLOCK, BLOCK), :] = x[:, pl.ds(i * BLOCK, BLOCK)].T

    def one(fn, *args):
        return (fn, *args)

    def two(fn, *args):
        return (both, fn, *args)

    steps = [
        one(wait_load, "x"),
        one(start_gate),
        two(compute, 1), two(start_sends, 1),
        two(s1, 0),
        one(wait_load, "dy"),
        two(compute, 2),
        two(s1, 1), two(s2, 0), two(start_sends, 2), two(s3, 0), two(s2, 1), two(s4, 0),
        two(s3, 1), two(s4, 1),
        two(make_hidden), two(s5, 0),
        two(s1, 2), two(s6, 0), two(s7, 0, 0), two(s2, 2), two(s7, 0, 1), two(s3, 2), two(s8, 0, 0),
        two(s4, 2),
        two(make_grads), two(s5, 1), two(s5, 2), two(s8, 0, 1), two(s6, 1), two(s6, 2),
        two(s7, 1, 0), two(s7, 2, 0),
        two(s9, 0, 0), two(s9, 0, 1),
        one(out_part),
        two(s8, 1, 0), two(s7, 1, 1),
        one(transpose_x),
        two(s8, 2, 0), two(s7, 2, 1),
        one(grad_down, 0),
        two(s9, 1, 0),
        one(dx_part, 1, 0),
        two(s8, 1, 1),
        two(s9, 2, 0),
        one(dx_part, 2, 0),
        two(s8, 2, 1),
        one(grad_down, 1),
        two(s9, 1, 1),
        one(dx_part, 1, 1),
        two(s9, 2, 1),
        one(dx_part, 2, 1),
        two(grad_cols, 0),
        one(finish_out),
        two(finish_grad, 2),
        two(grad_cols, 1),
        two(finish_grad, 0),
        one(finish_dx, 0),
        two(finish_grad, 1),
        one(finish_dx, 1),
    ]
    for fn, *args in steps:
        fn(*args)
    for key, cp in sent.items():
        if key not in got:
            cp.wait_recv()
        if key[0] != "d" or key not in got:
            cp.wait_send()
    for key in loads:
        if key not in loaded:
            loads[key].wait()


N_SENDS = 3 * 2 * 2 * 6 + 3 * 2 * 3 * 4 + 3 * (NZ - 1) + 6


def move(*refs):
    copies = [pltpu.make_async_copy(refs[k], refs[5 + k], refs[10].at[k]) for k in range(5)]
    for cp in copies:
        cp.start()
    for cp in copies:
        cp.wait()


def body(tokens, out_grad, gate_weight, up_weight, down_weight, gate_mask, up_mask, down_mask):
    hbm = pl.BlockSpec(memory_space=pltpu.HBM)
    smem = pl.BlockSpec(memory_space=pltpu.SMEM)
    vmem = pl.BlockSpec(memory_space=pltpu.VMEM)
    shapes = ((ZROWS, DIM), (ZROWS, DIM), (DIM, FF), (DIM, FF), (FF, DIM))
    results = tuple(jax.ShapeDtypeStruct(shape, BF16) for shape in shapes)
    made = pl.pallas_call(
        kernel,
        out_shape=results,
        in_specs=[hbm] * 5 + [smem] * 3,
        out_specs=(vmem,) * 5,
        scratch_shapes=[
            pltpu.VMEM((TOK, DIM), BF16),
            pltpu.VMEM((TOK, DIM), BF16),
            pltpu.VMEM((DIM, TOK), BF16),
            pltpu.VMEM((2, 2, DIM, HALF), BF16),
            pltpu.VMEM((2, HALF, DIM), BF16),
            pltpu.VMEM((3, 2, TOK, HALF), BF16),
            pltpu.VMEM((3, 2, BIG, HALF), BF16),
            pltpu.VMEM((3, 2, 2, BIG // 2, HALF), BF16),
            pltpu.VMEM((3, 2, 2, BIG, HALF), BF16),
            pltpu.VMEM((3, 2, 2, 32, HALF), BF16),
            pltpu.VMEM((3, 2, 2, SMALL, HALF), BF16),
            pltpu.VMEM((3, 2, SMALL, HALF), F32),
            pltpu.VMEM((3, 2, 4, 2, 2, SMALL, HALF), BF16),
            pltpu.VMEM((2, 2, DIM, HALF), BF16),
            pltpu.VMEM((2, HALF, DIM), BF16),
            pltpu.VMEM((TOK, DIM), BF16),
            pltpu.VMEM((NZ - 1, ZROWS, DIM), BF16),
            pltpu.VMEM((2, NZ, 48, DIM), BF16),
            pltpu.VMEM((2, NZ - 1, 48, DIM), BF16),
            pltpu.VMEM((TOK // 2, DIM), F32),
            pltpu.SemaphoreType.DMA((N_SENDS,)),
            pltpu.SemaphoreType.DMA((N_SENDS,)),
            pltpu.SemaphoreType.DMA((8,)),
        ],
        compiler_params=pltpu.CompilerParams(
            collective_id=0, has_side_effects=True, vmem_limit_bytes=VMEM_LIMIT
        ),
    )(tokens, out_grad, gate_weight, up_weight, down_weight, gate_mask, up_mask, down_mask.T)
    return pl.pallas_call(
        move,
        out_shape=results,
        in_specs=[vmem] * 5,
        out_specs=[hbm] * 5,
        scratch_shapes=[pltpu.SemaphoreType.DMA((5,))],
        compiler_params=pltpu.CompilerParams(vmem_limit_bytes=1 << 20),
    )(*made)


def solution(mesh):
    placed = (
        P("dp", "row"),
        P("dp", "row"),
        P("row", "col"),
        P("row", "col"),
        P("col", "row"),
        P("row", "col"),
        P("row", "col"),
        P("col", "row"),
    )
    return jax.shard_map(
        body,
        mesh=mesh,
        in_specs=placed,
        out_specs=(
            P(("dp", "col"), "row"),
            P(("dp", "col"), "row"),
            P("row", "col"),
            P("row", "col"),
            P("col", "row"),
        ),
        check_vma=False,
    )
```

time: 138 us -> 126 us (0.913); the launches traced: 137 us -> 124 us
  Pallas kernels: 126 us -> 119 us
  local copies, waits for them, and re-layouts: 10.8 us -> 4.3 us
    pallas_call x1 -> x2, Pallas kernels: 126 us -> 119 us  [the longest x1 116 us: body(): pl.pallas_call(kernel, out_shape=results, in_specs=[hbm] * 5 + [smem] * 3...]
    unnamed x10, local copies, waits for them, and re-layouts: 10.8 us -> 4.3 us
where the time goes in v2:
time: 126 us; the launch traced here: 124 us
  Pallas kernels  119 us (94%)
  local copies, waits for them, and re-layouts  4.3 us (3%)
    pallas_call x1, Pallas kernels, body(): pl.pallas_call(kernel, out_shape=results, in_specs=[hbm] * 5 + [smem] * 3...  116 us
    unnamed x10, local copies, waits for them, and re-layouts  4.3 us
    pallas_call x1, Pallas kernels, body(): pl.pallas_call(move, out_shape=results, in_specs=[vmem] * 5, out_specs=[h...  2.55 us

profile of v2, /device:TPU:2, one launch (start us, length us, event | category | flops | bytes accessed | tf_op | source)
XLA Modules:
  0.0 123.8 jit_solution(8991496694643496245)
XLA Ops:
  0.6 0.0 copy-start
  0.6 1.1 copy-done
  1.8 0.0 copy-start.1
  1.8 1.1 copy-done.1
  2.9 0.0 copy-start.2
  2.9 0.7 copy-done.2
  3.6 0.0 copy-start.3
  3.6 0.7 copy-done.3
  4.3 0.0 copy-start.4
  4.3 0.7 copy-done.4
  4.9 116.3 %shard_map.119 = (bf16[96,512]{1,0:T(8,128)(2,1)S(1)}, bf16[96,512]{1,0:T(8,128)(2,1)S(1)}, bf16[512,1792]{1,0:T(8,128)(2,1)S(1)}, bf16[512,1792]{1,0:T(8,128)(2,1)S(1)}, bf16[1792,512]{1,0:T(8,128)(2,1)S(1)}) custom-call(bf16[768,512]{1,0:T(8,128)(2,1)S(1)} %copy-done, bf16[768,512]{1,0:T(8,128)(2,1)S(1)} %copy-done.1, bf16[512,1792]{1,0:T(8,128)(2,1)} %gw_hbm.1, ...), custom_call_target="tpu_custom_call" | custom-call | tf_op jit(solution)/shard_map/pallas_call | solution.py:487
  121.3 2.5 %shard_map.120 = (bf16[96,512]{1,0:T(8,128)(2,1)}, bf16[96,512]{1,0:T(8,128)(2,1)}, bf16[512,1792]{1,0:T(8,128)(2,1)}, bf16[512,1792]{1,0:T(8,128)(2,1)}, bf16[1792,512]{1,0:T(8,128)(2,1)}) custom-call(bf16[96,512]{1,0:T(8,128)(2,1)S(1)} %get-tuple-element.10.refs_0_, bf16[96,512]{1,0:T(8,128)(2,1)S(1)} %get-tuple-element.11.refs_1_, ...), custom_call_target="tpu_custom_call" | custom-call | tf_op jit(solution)/shard_map/pallas_call | solution.py:521
Async XLA Ops:
  0.6 1.1 copy-start
  1.8 1.1 copy-start.1
  2.9 0.7 copy-start.2
  3.6 0.7 copy-start.3
  4.3 0.7 copy-start.4
